TPU v7x, 128 devices: a whole 4x4x4 slice. The times are simulated.
128 devices in a mesh: gx: 16 (over z_lo, x, core), gz: 8 (over y, z_hi).
Axes of the slice: x: 4, y: 4, z: 4 (z_hi: 2, z_lo: 2; z = z_hi * 2 + z_lo), core: 2. Of those that a mesh axis runs over, the one named last changes fastest.
Arguments:
- elevation: float32 [2048, 2048], P(('gx', 'gz')), may hold values from -2 to 2
- potential: float32 [2048, 2048], P(('gx', 'gz')), may hold values from -6 to 6
- tracer: float32 [2048, 64, 256], P('gx', 'gz'), may hold values from -6 to 6
- wind_speed: float32 [2048, 64, 256], P('gx', 'gz'), may hold values from -4 to 4
Outputs:
- new_elevation: float32 [2048, 2048], P(('gx', 'gz'))
- new_tracer: float32 [2048, 64, 256], P('gx', 'gz')
All inputs are finite; a program needn't handle non-finite values.
Results may differ from a plain program's by a relative error of at most 0.00019.
Values sent between devices are 32-bit elements; how exact they have to be, the bound alone decides.
No kernel may reach another device: no remote copies, remote signals or barrier semaphores. Data moves between devices by JAX's collectives and lax.ppermute only.
A program may use at most 128 MiB of HBM per device.

v0:
```python
import jax
import jax.numpy as jnp
from jax import lax
from jax.sharding import PartitionSpec as P

NS = 2048
TWO_PI = 6.283185307179586
DT_WAVE = 0.05
COLUMN_DEPTH = 32.0
DT_AIR = 0.1
NU_AIR = 0.2
PRECISE = lax.Precision.HIGHEST


def padded_2(shard, sides, width, wrap):
    for axis, dim in sides:
        size, length = (lax.axis_size(axis), shard.shape[dim])
        up = [(i, (i + 1) % size) for i in range(size if wrap else size - 1)]
        down = [(j, i) for i, j in up]
        last = lax.slice_in_dim(shard, length - width, length, axis=dim)
        leading = lax.slice_in_dim(shard, 0, width, axis=dim)
        before = lax.ppermute(last, axis, up)
        after = lax.ppermute(leading, axis, down)
        shard = jnp.concatenate([before, shard, after], axis=dim)
    return shard


def angle_table(row_count, col_count, length):
    row_index = jnp.arange(row_count, dtype=jnp.int32)
    col_index = jnp.arange(col_count, dtype=jnp.int32)
    product = row_index[:, None] * col_index[None, :] % length
    angles = product.astype(jnp.float32) * (TWO_PI / length)
    return (jnp.cos(angles), jnp.sin(angles))


def contract(pattern, real_part, imaginary, cosine, sine, sign_value, keep_imaginary):
    real_cosine = jnp.einsum(pattern, real_part, cosine, precision=PRECISE)
    real_sine = jnp.einsum(pattern, real_part, sine, precision=PRECISE)
    if imaginary is None:
        return (real_cosine, sign_value * real_sine)
    imag_sine = jnp.einsum(pattern, imaginary, sine, precision=PRECISE)
    out_real = real_cosine - sign_value * imag_sine
    if not keep_imaginary:
        return (out_real, None)
    imag_cosine = jnp.einsum(pattern, imaginary, cosine, precision=PRECISE)
    return (out_real, imag_cosine + sign_value * real_sine)


def twist_phase(real_part, imaginary, cosine, sine, sign_value):
    out_real = real_part * cosine - sign_value * imaginary * sine
    out_imag = imaginary * cosine + sign_value * real_part * sine
    return (out_real, out_imag)


def transform_last(real_part, imaginary, inverse, keep_imaginary):
    length = real_part.shape[-1]
    inner_size = 128
    outer_size = length // inner_size
    leading = real_part.shape[:-1]
    sign_value = 1.0 if inverse else -1.0
    cosine_outer, sine_outer = angle_table(outer_size, outer_size, outer_size)
    cosine_inner, sine_inner = angle_table(inner_size, inner_size, inner_size)
    cosine_twist, sine_twist = angle_table(outer_size, inner_size, length)
    real_part = real_part.reshape(leading + (outer_size, inner_size))
    if imaginary is not None:
        imaginary = imaginary.reshape(leading + (outer_size, inner_size))
    if not inverse:
        real_part, imaginary = contract(
            "...an,ak->...kn", real_part, imaginary, cosine_outer, sine_outer, sign_value, True
        )
        real_part, imaginary = twist_phase(
            real_part, imaginary, cosine_twist, sine_twist, sign_value
        )
        real_part, imaginary = contract(
            "...kn,nb->...kb", real_part, imaginary, cosine_inner, sine_inner, sign_value, True
        )
        return (real_part.reshape(leading + (length,)), imaginary.reshape(leading + (length,)))
    real_part, imaginary = contract(
        "...kb,bn->...kn", real_part, imaginary, cosine_inner, sine_inner, sign_value, True
    )
    real_part, imaginary = twist_phase(real_part, imaginary, cosine_twist, sine_twist, sign_value)
    real_part, imaginary = contract(
        "...kn,ka->...an",
        real_part,
        imaginary,
        cosine_outer,
        sine_outer,
        sign_value,
        keep_imaginary,
    )
    factor = 1.0 / length
    real_part = real_part.reshape(leading + (length,)) * factor
    if imaginary is None:
        return (real_part, None)
    return (real_part, imaginary.reshape(leading + (length,)) * factor)


def permuted_waves(positions, length):
    inner_size = 128
    outer_size = length // inner_size
    wave_index = positions // inner_size + outer_size * (positions % inner_size)
    signed = jnp.where(wave_index < length // 2, wave_index, wave_index - length).astype(
        jnp.float32
    ) * (TWO_PI / length)
    odd_wave = jnp.where(wave_index == length // 2, 0.0, signed)
    return (signed, odd_wave)


def block_start(block_rows):
    return (lax.axis_index("gx") * lax.axis_size("gz") + lax.axis_index("gz")) * block_rows


def to_columns(stacked):
    return lax.all_to_all(stacked, ("gx", "gz"), split_axis=3, concat_axis=2, tiled=True)


def to_rows(stacked):
    return lax.all_to_all(stacked, ("gx", "gz"), split_axis=2, concat_axis=3, tiled=True)


def spectra(fields):
    real_part, imaginary = transform_last(fields, None, False, True)
    stacked = jnp.stack([real_part, imaginary], 1)
    turned = jnp.swapaxes(to_columns(stacked), 2, 3)
    return transform_last(turned[:, 0], turned[:, 1], False, True)


def fields_back(real_part, imaginary):
    real_part, imaginary = transform_last(real_part, imaginary, True, True)
    stacked = jnp.swapaxes(jnp.stack([real_part, imaginary], 1), 2, 3)
    turned = to_rows(stacked)
    return transform_last(turned[:, 0], turned[:, 1], True, False)


def fields_from(spectrum_list):
    members = len(spectrum_list)
    real_part, unused = fields_back(
        jnp.stack([member[0] for member in spectrum_list]),
        jnp.stack([member[1] for member in spectrum_list]),
    )
    return [real_part[offset] for offset in range(members)]


def scaled(real_part, imaginary, factor):
    return (factor * real_part, factor * imaginary)


def derived(real_part, imaginary, factor):
    return (-factor * imaginary, factor * real_part)


def level_rims(field):
    padded = padded_2(field, (("gz", 1),), 1, False)
    bottom = lax.axis_index("gz") == 0
    top_device = lax.axis_index("gz") == lax.axis_size("gz") - 1
    lower_level = jnp.concatenate(
        [jnp.where(bottom, field[:, :1], padded[:, :1]), field[:, :-1]], 1
    )
    upper_level = jnp.concatenate(
        [field[:, 1:], jnp.where(top_device, field[:, -1:], padded[:, -1:])], 1
    )
    return (lower_level, upper_level)


def shards(elevation, potential, tracer, wind_speed):
    block_rows = elevation.shape[0]
    real_part, imaginary = spectra(jnp.stack([elevation, potential]))
    positions = block_start(block_rows) + jnp.arange(block_rows, dtype=jnp.int32)
    wave_y, odd_y = permuted_waves(positions, NS)
    wave_x, odd_x = permuted_waves(jnp.arange(NS, dtype=jnp.int32), NS)
    magnitude = jnp.sqrt(wave_x[None, :] * wave_x[None, :] + wave_y[:, None] * wave_y[:, None])
    squared = magnitude * magnitude
    magnitude_cube = squared * magnitude
    along_x = odd_x[None, :] + jnp.zeros_like(magnitude)
    along_y = odd_y[:, None] + jnp.zeros_like(magnitude)
    eta_real, eta_imag = (real_part[0], imaginary[0])
    phi_real, phi_imag = (real_part[1], imaginary[1])
    first_once, first_twice, first_thrice, slope_x, slope_y, speed_x, speed_y = fields_from(
        [
            scaled(phi_real, phi_imag, magnitude),
            scaled(phi_real, phi_imag, squared),
            scaled(phi_real, phi_imag, magnitude_cube),
            derived(eta_real, eta_imag, along_x),
            derived(eta_real, eta_imag, along_y),
            derived(phi_real, phi_imag, along_x),
            derived(phi_real, phi_imag, along_y),
        ]
    )
    second_field = -elevation * first_once
    real_part, imaginary = spectra(second_field[None])
    second_once, second_twice = fields_from(
        [scaled(real_part[0], imaginary[0], magnitude), scaled(real_part[0], imaginary[0], squared)]
    )
    third_field = -elevation * second_once - 0.5 * elevation * elevation * first_twice
    real_part, imaginary = spectra(third_field[None])
    third_list = fields_from([scaled(real_part[0], imaginary[0], magnitude)])
    third_once = third_list[0]
    vertical = (
        first_once
        + elevation * first_twice
        + 0.5 * elevation * elevation * first_thrice
        + second_once
        + elevation * second_twice
        + third_once
    )
    tendency = (
        -(slope_x * speed_x + slope_y * speed_y)
        + (1.0 + slope_x * slope_x + slope_y * slope_y) * vertical
    )
    new_elevation = elevation + DT_WAVE * tendency
    columns = tracer.shape[2]
    padded = padded_2(tracer, (("gx", 0),), 1, True)
    eastern = padded[2:]
    western = padded[:-2]
    northern = jnp.concatenate([tracer[:, :, 1:], tracer[:, :, -1:]], 2)
    southern = jnp.concatenate([tracer[:, :, :1], tracer[:, :, :-1]], 2)
    moved_tracer = tracer + DT_AIR * (
        -wind_speed * (eastern - western) * 0.5
        + NU_AIR * (eastern + western + northern + southern - 4.0 * tracer)
    )
    real_part, imaginary = spectra(new_elevation[None])
    slope_list = fields_from([derived(real_part[0], imaginary[0], along_x)])
    new_slope = slope_list[0]
    window = jnp.stack([elevation[:, :columns], new_elevation[:, :columns], new_slope[:, :columns]])
    surface = lax.all_gather(window, "gz", axis=1, tiled=True)
    old_rows = surface[0]
    new_rows = surface[1]
    slope_rows = surface[2]
    levels = tracer.shape[1]
    level_count = levels * lax.axis_size("gz")
    sigma_level = (
        (lax.axis_index("gz") * levels + jnp.arange(levels, dtype=jnp.int32)).astype(jnp.float32)
        + 0.5
    ) / level_count
    lift_factor = (1.0 - sigma_level)[None, :, None]
    level_shift = (
        ((new_rows - old_rows) / (COLUMN_DEPTH - old_rows))[:, None, :] * lift_factor * level_count
    )
    lower_level, upper_level = level_rims(moved_tracer)
    remapped = (
        moved_tracer
        + 0.5 * level_shift * (upper_level - lower_level)
        + 0.5 * level_shift * level_shift * (upper_level - 2.0 * moved_tracer + lower_level)
    )
    lower_level, upper_level = level_rims(remapped)
    column_depth = (COLUMN_DEPTH - new_rows)[:, None, :]
    advection = (
        wind_speed
        * lift_factor
        * slope_rows[:, None, :]
        / column_depth
        * (upper_level - lower_level)
        * (0.5 * level_count)
    )
    spread_term = (
        NU_AIR
        * (upper_level - 2.0 * remapped + lower_level)
        * (level_count * level_count)
        / (column_depth * column_depth)
    )
    new_tracer = remapped + DT_AIR * (advection + spread_term)
    return (new_elevation, new_tracer)


def solution(mesh):
    return jax.shard_map(
        shards,
        mesh=mesh,
        in_specs=(
            P(("gx", "gz"), None),
            P(("gx", "gz"), None),
            P("gx", "gz", None),
            P("gx", "gz", None),
        ),
        out_specs=(P(("gx", "gz"), None), P("gx", "gz", None)),
        check_vma=False,
    )
```

profile of v0, /device:TPU:8, one launch (start us, length us, event | category | flops | bytes accessed | tf_op | source)
XLA Modules:
  0.0 606.4 jit_solution(7506074649540263558)
XLA Ops:
  10.3 7.0 %fusion.923 = f32[2048,2,2,16]{3,2,1,0:T(2,128)} fusion(f32[2,1,16,2048]{2,1,0,3:T(1,128)} %bitcast.800, f32[2,1,16,2048]{2,1,0,3:T(1,128)S(1)} %bitcast.798), kind=kLoop, calls=%fused_computation.1021 | loop fusion | flops 131072 | bytes 1048576
  17.3 8.0 %reshape.1070 = f32[128,1,1024]{2,1,0:T(1,128)} reshape(f32[2048,2,2,16]{3,2,1,0:T(2,128)} %fusion.923) | data formatting | bytes 1048576
  25.3 10.8 %all-to-all-start = ((f32[128,1,1024]{2,1,0:T(1,128)}), f32[128,1,1024]{2,1,0:T(1,128)S(1)}, u32[]{:S(2)}, u32[]{:S(2)}) async-start(f32[128,1,1024]{2,1,0:T(1,128)} %reshape.1070), calls=%async_computation | async-start | bytes 1048576 | tf_op jit(solution)/shard_map/all_to_all | solution.py:114
  36.1 12.8 %all-to-all-done = f32[128,1,1024]{2,1,0:T(1,128)S(1)} async-done(((f32[128,1,1024]{2,1,0:T(1,128)}), f32[128,1,1024]{2,1,0:T(1,128)S(1)}, u32[]{:S(2)}, u32[]{:S(2)}) %all-to-all-start) | async-done | bytes 524320 | tf_op jit(solution)/shard_map/all_to_all | solution.py:114
  51.5 6.9 %reshape.1071 = f32[2048,2,2,16]{3,2,1,0:T(2,128)} reshape(f32[128,1024]{1,0:T(8,128)S(1)} %reduce) | data formatting | bytes 1048576
  58.5 6.6 %copy.542 = f32[2,2,16,128,16]{2,3,4,1,0:T(8,128)} copy(f32[2,2,16,128,16]{2,1,0,4,3:T(2,128)} %bitcast.781) | data formatting | bytes 1048576 | tf_op jit(solution)/shard_map/all_to_all | solution.py:114
  65.1 4.9 all_to_all.107
  84.8 16.8 %copy.276 = f32[7,1,16,2048]{2,1,0,3:T(1,128)} copy(f32[7,1,16,2048]{3,2,0,1:T(8,128)} %mul.3195) | data formatting | bytes 1835008 | tf_op jit(solution)/shard_map/mul | solution.py:92
  103.9 12.4 %copy.277 = f32[7,1,16,2048]{2,1,0,3:T(1,128)} copy(f32[7,1,16,2048]{3,2,0,1:T(8,128)S(1)} %mul.3198) | data formatting | bytes 1835008 | tf_op jit(solution)/shard_map/mul | solution.py:95
  116.3 19.0 %fusion.921 = f32[2048,7,2,16]{3,2,1,0:T(2,128)} fusion(f32[7,1,16,2048]{2,1,0,3:T(1,128)} %copy.277, f32[7,1,16,2048]{2,1,0,3:T(1,128)} %copy.276), kind=kLoop, calls=%fused_computation.1019 | loop fusion | flops 458752 | bytes 3670016
  135.4 22.7 %reshape.1072 = f32[128,1,3584]{2,1,0:T(1,128)} reshape(f32[2048,7,2,16]{3,2,1,0:T(2,128)} %fusion.921) | data formatting | bytes 3670016
  158.1 31.8 %all_to_all.144 = f32[128,1,3584]{2,1,0:T(1,128)S(1)} all-to-all(f32[128,1,3584]{2,1,0:T(1,128)} %reshape.1072), channel_id=1, replica_groups=mesh['gx'=16,'gz'=8] {'gx','gz'}, dimensions={0} | all-to-all | bytes 3670016 | tf_op jit(solution)/shard_map/all_to_all | solution.py:118
  189.9 6.7 %reduce.1 = f32[128,3584]{1,0:T(8,128)} reduce(f32[128,1,3584]{2,1,0:T(1,128)S(1)} %all_to_all.144, f32[]{:T(128)} %broadcast.1810), dimensions={1}, to_apply=%all_to_all.108.reduce_sub_computation | reduce | bytes 3670020 | tf_op jit(solution)/shard_map/all_to_all | solution.py:118
  196.6 22.7 %reshape.1073 = f32[2048,7,2,16]{3,2,1,0:T(2,128)} reshape(f32[128,3584]{1,0:T(8,128)} %reduce.1) | data formatting | bytes 3670016
  219.3 18.8 %copy.540 = f32[7,2,128,16,16]{4,2,3,1,0:T(8,128)} copy(f32[7,2,128,16,16]{4,1,0,3,2:T(2,128)} %bitcast.779) | data formatting | bytes 3670016 | tf_op jit(solution)/shard_map/all_to_all | solution.py:118
  238.1 13.0 %all_to_all.111 = f32[7,2,16,2048]{3,2,1,0:T(8,128)S(1)} reshape(f32[7,2,16,128,16]{4,3,2,1,0:T(8,128)} %bitcast.780) | data formatting | bytes 3670016 | tf_op jit(solution)/shard_map/all_to_all | solution.py:118
  262.9 3.6 reshape.1074
  266.5 5.2 all-to-all-start.2
  272.4 3.6 collective-permute-start
  278.3 3.7 all-to-all-done.2
  283.4 4.1 reshape.1075
  287.5 4.1 copy.547
  291.7 3.1 all_to_all.115
  306.3 7.4 %fusion.922 = f32[2048,2,2,16]{3,2,1,0:T(2,128)} fusion(f32[2,1,16,2048]{2,1,0,3:T(1,128)} %bitcast.801, f32[2,1,16,2048]{2,1,0,3:T(1,128)} %bitcast.799), kind=kLoop, calls=%fused_computation.1020 | loop fusion | flops 131072 | bytes 1048576
  313.7 8.0 %reshape.1076 = f32[128,1,1024]{2,1,0:T(1,128)} reshape(f32[2048,2,2,16]{3,2,1,0:T(2,128)} %fusion.922) | data formatting | bytes 1048576
  321.6 6.1 %all-to-all-start.3 = ((f32[128,1,1024]{2,1,0:T(1,128)}), f32[128,1,1024]{2,1,0:T(1,128)S(1)}, u32[]{:S(2)}, u32[]{:S(2)}) async-start(f32[128,1,1024]{2,1,0:T(1,128)} %reshape.1076), calls=%async_computation.3 | async-start | bytes 1048576 | tf_op jit(solution)/shard_map/all_to_all | solution.py:118
  330.0 10.7 %all-to-all-done.3 = f32[128,1,1024]{2,1,0:T(1,128)S(1)} async-done(((f32[128,1,1024]{2,1,0:T(1,128)}), f32[128,1,1024]{2,1,0:T(1,128)S(1)}, u32[]{:S(2)}, u32[]{:S(2)}) %all-to-all-start.3) | async-done | bytes 524320 | tf_op jit(solution)/shard_map/all_to_all | solution.py:118
  342.7 6.9 %reshape.1077 = f32[2048,2,2,16]{3,2,1,0:T(2,128)} reshape(f32[128,1024]{1,0:T(8,128)S(1)} %reduce.3) | data formatting | bytes 1048576
  349.6 6.6 %copy.541 = f32[2,2,128,16,16]{4,2,3,1,0:T(8,128)} copy(f32[2,2,128,16,16]{4,1,0,3,2:T(2,128)} %bitcast.783) | data formatting | bytes 1048576 | tf_op jit(solution)/shard_map/all_to_all | solution.py:118
  356.2 5.2 all_to_all.119
  368.6 2.3 copy.307
  370.9 5.0 reshape.1078
  375.9 5.0 all-to-all-start.4
  382.1 9.2 %all-to-all-done.4 = f32[128,1,512]{2,1,0:T(1,128)S(1)} async-done(((f32[128,1,512]{2,1,0:T(1,128)}), f32[128,1,512]{2,1,0:T(1,128)S(1)}, u32[]{:S(2)}, u32[]{:S(2)}) %all-to-all-start.4) | async-done | bytes 262176 | tf_op jit(solution)/shard_map/all_to_all | solution.py:114
  392.6 4.1 reshape.1079
  396.8 4.1 copy.546
  400.9 3.1 all_to_all.123
  413.3 2.6 bitcast_bitcast_fusion.1
  415.9 5.4 reshape.1080
  421.3 5.8 all-to-all-start.5
  427.2 2.8 fusion.48
  430.7 5.3 collective-permute-start.2
  440.3 4.1 reshape.1081
  444.5 4.1 copy.545
  448.6 3.1 all_to_all.127
  458.0 2.5 copy.338
  460.5 5.0 reshape.1082
  465.5 11.2 %all-to-all-start.6 = ((f32[128,1,512]{2,1,0:T(1,128)}), f32[128,1,512]{2,1,0:T(1,128)}, u32[]{:S(2)}, u32[]{:S(2)}) async-start(f32[128,1,512]{2,1,0:T(1,128)} %reshape.1082), calls=%async_computation.6 | async-start | bytes 524288 | tf_op jit(solution)/shard_map/all_to_all | solution.py:114
  477.8 9.0 %all-to-all-done.6 = f32[128,1,512]{2,1,0:T(1,128)} async-done(((f32[128,1,512]{2,1,0:T(1,128)}), f32[128,1,512]{2,1,0:T(1,128)}, u32[]{:S(2)}, u32[]{:S(2)}) %all-to-all-start.6) | async-done | bytes 262176 | tf_op jit(solution)/shard_map/all_to_all | solution.py:114
  486.8 3.0 reduce.6
  489.7 5.1 reshape.1083
  494.8 4.1 copy.544
  498.9 3.8 all_to_all.131
  516.1 2.6 bitcast_bitcast_fusion
  518.7 5.2 reshape.1084
  523.9 5.8 all-to-all-start.7
  532.7 7.1 %all-to-all-done.7 = f32[128,1,512]{2,1,0:T(1,128)} async-done(((f32[128,1,512]{2,1,0:T(1,128)}), f32[128,1,512]{2,1,0:T(1,128)}, u32[]{:S(2)}, u32[]{:S(2)}) %all-to-all-start.7) | async-done | bytes 262176 | tf_op jit(solution)/shard_map/all_to_all | solution.py:118
  542.1 4.1 reshape.1085
  546.3 4.1 copy.543
  550.4 3.1 all_to_all.135
  556.5 33.7 %all_gather.3 = f32[3,128,256]{2,1,0:T(8,128)S(1)} all-gather(f32[3,16,256]{2,1,0:T(8,128)S(1)} %pad_maximum_fusion.14), channel_id=1, replica_groups=mesh['gx'=16,'gz'=8] {'gz'}, dimensions={1}, use_global_device_ids=true | all-gather | bytes 442368 | tf_op jit(solution)/shard_map/all_gather | solution.py:225
  591.0 3.2 collective-permute-start.4
  594.2 4.1 collective-permute-start.5
  599.4 4.2 collective-permute-done.5
  (268 shorter events, 116.6 us)
Async XLA Ops:
  25.3 23.7 %all-to-all-start = ((f32[128,1,1024]{2,1,0:T(1,128)}), f32[128,1,1024]{2,1,0:T(1,128)S(1)}, u32[]{:S(2)}, u32[]{:S(2)}) async-start(f32[128,1,1024]{2,1,0:T(1,128)} %reshape.1070), calls=%async_computation | async-start | bytes 1048576 | tf_op jit(solution)/shard_map/all_to_all | solution.py:114
  257.0 1.8 copy-start.2
  258.8 106.8 %copy-start.3 = (f32[1,16,16,128]{3,2,1,0:T(8,128)}, f32[1,16,16,128]{3,2,1,0:T(8,128)S(1)}, u32[]{:S(2)}) copy-start(f32[1,16,16,128]{3,2,1,0:T(8,128)S(1)} %get-tuple-element.32) | copy-start | bytes 393220
  266.5 15.6 %all-to-all-start.2 = ((f32[128,1,512]{2,1,0:T(1,128)}), f32[128,1,512]{2,1,0:T(1,128)S(1)}, u32[]{:S(2)}, u32[]{:S(2)}) async-start(f32[128,1,512]{2,1,0:T(1,128)} %reshape.1074), calls=%async_computation.2 | async-start | bytes 524288 | tf_op jit(solution)/shard_map/all_to_all | solution.py:114
  272.4 154.8 %collective-permute-start = (f32[1,8,256]{2,0,1:T(1,128)S(1)}, f32[1,8,256]{2,0,1:T(1,128)S(1)}, u32[]{:S(2)}, u32[]{:S(2)}) collective-permute-start(f32[1,8,256]{2,0,1:T(1,128)S(1)} %copy.322), channel_id=1, source_target_pairs={{8,0},{16,8},{24,16},{32,24},{40,32},{48,40},{56,48},{64,56},{72,6... | collective-permute-start | bytes 24584 | tf_op jit(solution)/shard_map/ppermute | solution.py:23
  276.0 151.2 %collective-permute-start.1 = (f32[1,8,256]{2,0,1:T(1,128)S(1)}, f32[1,8,256]{2,0,1:T(1,128)S(1)}, u32[]{:S(2)}, u32[]{:S(2)}) collective-permute-start(f32[1,8,256]{2,0,1:T(1,128)S(1)} %copy.324), channel_id=1, source_target_pairs={{0,8},{8,16},{16,24},{24,32},{32,40},{40,48},{48,56},{56,64},{64,7... | collective-permute-start | bytes 24584 | tf_op jit(solution)/shard_map/ppermute | solution.py:22
  321.6 19.1 %all-to-all-start.3 = ((f32[128,1,1024]{2,1,0:T(1,128)}), f32[128,1,1024]{2,1,0:T(1,128)S(1)}, u32[]{:S(2)}, u32[]{:S(2)}) async-start(f32[128,1,1024]{2,1,0:T(1,128)} %reshape.1076), calls=%async_computation.3 | async-start | bytes 1048576 | tf_op jit(solution)/shard_map/all_to_all | solution.py:118
  365.5 3.1 copy-start.5
  375.9 15.4 %all-to-all-start.4 = ((f32[128,1,512]{2,1,0:T(1,128)}), f32[128,1,512]{2,1,0:T(1,128)S(1)}, u32[]{:S(2)}, u32[]{:S(2)}) async-start(f32[128,1,512]{2,1,0:T(1,128)} %reshape.1078), calls=%async_computation.4 | async-start | bytes 524288 | tf_op jit(solution)/shard_map/all_to_all | solution.py:114
  415.9 11.2 %copy-start = (f32[128,8,256]{2,1,0:T(8,128)S(1)}, f32[128,8,256]{2,1,0:T(8,128)}, u32[]{:S(2)}) copy-start(f32[128,8,256]{2,1,0:T(8,128)} %param.7) | copy-start | bytes 3145732
  421.3 16.7 %all-to-all-start.5 = ((f32[128,1,512]{2,1,0:T(1,128)}), f32[128,1,512]{2,1,0:T(1,128)}, u32[]{:S(2)}, u32[]{:S(2)}) async-start(f32[128,1,512]{2,1,0:T(1,128)} %reshape.1080), calls=%async_computation.5 | async-start | bytes 524288 | tf_op jit(solution)/shard_map/all_to_all | solution.py:118
  430.7 99.0 %collective-permute-start.2 = (f32[128,1,256]{2,0,1:T(8,128)}, f32[128,1,256]{2,0,1:T(8,128)}, u32[]{:S(2)}, u32[]{:S(2)}) collective-permute-start(f32[128,1,256]{2,0,1:T(8,128)} %get-tuple-element.20), channel_id=1, source_target_pairs={{1,0},{2,1},{3,2},{4,3},{5,4},{6,5},{7,6},{9,8},{10,9},{11,10},{12... | collective-permute-start | bytes 393224 | tf_op jit(solution)/shard_map/ppermute | solution.py:23
  436.0 93.7 %collective-permute-start.3 = (f32[128,1,256]{2,0,1:T(8,128)}, f32[128,1,256]{2,0,1:T(8,128)}, u32[]{:S(2)}, u32[]{:S(2)}) collective-permute-start(f32[128,1,256]{2,0,1:T(8,128)} %get-tuple-element.21), channel_id=1, source_target_pairs={{0,1},{1,2},{2,3},{3,4},{4,5},{5,6},{6,7},{8,9},{9,10},{10,11},{11... | collective-permute-start | bytes 393224 | tf_op jit(solution)/shard_map/ppermute | solution.py:22
  451.7 2.9 copy-start.4
  451.7 2.9 copy-start.6
  451.7 2.9 copy-start.8
  451.7 2.9 copy-start.9
  451.8 2.9 copy-start.10
  451.8 2.9 copy-start.11
  455.0 0.7 copy-start.7
  465.5 21.3 %all-to-all-start.6 = ((f32[128,1,512]{2,1,0:T(1,128)}), f32[128,1,512]{2,1,0:T(1,128)}, u32[]{:S(2)}, u32[]{:S(2)}) async-start(f32[128,1,512]{2,1,0:T(1,128)} %reshape.1082), calls=%async_computation.6 | async-start | bytes 524288 | tf_op jit(solution)/shard_map/all_to_all | solution.py:114
  523.9 16.0 %all-to-all-start.7 = ((f32[128,1,512]{2,1,0:T(1,128)}), f32[128,1,512]{2,1,0:T(1,128)}, u32[]{:S(2)}, u32[]{:S(2)}) async-start(f32[128,1,512]{2,1,0:T(1,128)} %reshape.1084), calls=%async_computation.7 | async-start | bytes 524288 | tf_op jit(solution)/shard_map/all_to_all | solution.py:118
  553.6 2.9 copy-start.13
  553.6 2.9 copy-start.14
  553.6 36.6 %copy-start.1 = (f32[128,7,256]{2,0,1:T(8,128)S(1)}, f32[128,7,256]{2,0,1:T(8,128)}, u32[]{:S(2)}) copy-start(f32[128,7,256]{2,0,1:T(8,128)} %get-tuple-element.17) | copy-start | bytes 2752516
  553.6 36.6 %copy-start.12 = (f32[128,1,256]{2,0,1:T(8,128)S(1)}, f32[128,1,256]{2,0,1:T(8,128)}, u32[]{:S(2)}) copy-start(f32[128,1,256]{2,0,1:T(8,128)} %get-tuple-element.19) | copy-start | bytes 393220
  553.6 36.6 %copy-start.15 = (f32[8]{0:T(128)S(1)}, f32[8]{0:T(128)}, u32[]{:S(2)}) copy-start(f32[8]{0:T(128)} %multiply_subtract_fusion.18) | copy-start | bytes 100
  591.0 8.4 %collective-permute-start.4 = (f32[128,1,256]{2,0,1:T(8,128)S(1)}, f32[128,1,256]{2,0,1:T(8,128)S(1)}, u32[]{:S(2)}, u32[]{:S(2)}) collective-permute-start(f32[128,1,256]{2,0,1:T(8,128)S(1)} %get-tuple-element.14), channel_id=1, source_target_pairs={{1,0},{2,1},{3,2},{4,3},{5,4},{6,5},{7,6},{9,8},{10,9},{11,10},{12... | collective-permute-start | bytes 393224 | tf_op jit(solution)/shard_map/ppermute | solution.py:23
  594.2 9.3 %collective-permute-start.5 = (f32[128,1,256]{2,0,1:T(8,128)S(1)}, f32[128,1,256]{2,0,1:T(8,128)S(1)}, u32[]{:S(2)}, u32[]{:S(2)}) collective-permute-start(f32[128,1,256]{2,0,1:T(8,128)S(1)} %get-tuple-element.15), channel_id=1, source_target_pairs={{0,1},{1,2},{2,3},{3,4},{4,5},{5,6},{6,7},{8,9},{9,10},{10,11},{11... | collective-permute-start | bytes 393224 | tf_op jit(solution)/shard_map/ppermute | solution.py:22
where the time goes:
time: 617 us; the launch traced here: 606 us
  local copies, waits for them, and re-layouts  285 us (46%)
  starting transfers between devices  68.5 us (11%)
  blocking collectives  65.5 us (11%)
  matrix products  63.7 us (10%)
  other arithmetic  63 us (10%)
  waiting for transfers between devices  57.8 us (9%)
    unnamed x80, local copies, waits for them, and re-layouts  133 us
    all_to_all x8, local copies, waits for them, and re-layouts, to_rows(): lax.all_to_all(stacked, ('gx', 'gz'), split_axis=2, concat_axis=3, tiled=...  58.2 us
    all_to_all x4, waiting for transfers between devices, to_columns(): lax.all_to_all(stacked, ('gx', 'gz'), split_axis=3, concat_axis=2, tiled=...  34.8 us
    all_to_all x9, local copies, waits for them, and re-layouts, to_columns(): lax.all_to_all(stacked, ('gx', 'gz'), split_axis=3, concat_axis=2, tiled=...  34.7 us
    unnamed x15, other arithmetic  34.3 us
    all_gather x1, blocking collectives, shards(): surface = lax.all_gather(window, 'gz', axis=1, tiled=True)  33.7 us
    all_to_all x4, starting transfers between devices, to_columns(): lax.all_to_all(stacked, ('gx', 'gz'), split_axis=3, concat_axis=2, tiled=...  32.1 us
    all_to_all x1, blocking collectives, to_rows(): lax.all_to_all(stacked, ('gx', 'gz'), split_axis=2, concat_axis=3, tiled=...  31.8 us
  transfers between devices with their start and end apart: 13, of which 8 were waited for; matrix products, arithmetic and copies ran while one was open for 27% of the time, Pallas kernels for 0%

commit v1 on v0

--- a/solution.py
+++ b/solution.py
@@ -222,7 +222,9 @@
     slope_list = fields_from([derived(real_part[0], imaginary[0], along_x)])
     new_slope = slope_list[0]
     window = jnp.stack([elevation[:, :columns], new_elevation[:, :columns], new_slope[:, :columns]])
-    surface = lax.all_gather(window, "gz", axis=1, tiled=True)
+    surface = jnp.concatenate(
+        lax.all_to_all(jnp.stack(lax.axis_size("gz") * [window], 0), "gz", 0, 0), axis=1
+    )
     old_rows = surface[0]
     new_rows = surface[1]
     slope_rows = surface[2]

time: 617 us -> 579 us (0.938)
  blocking collectives: 65.5 us -> 47.4 us
  local copies, waits for them, and re-layouts: 285 us -> 276 us
  starting transfers between devices: 68.5 us -> 60.3 us
    all_gather x1 -> x0, blocking collectives: 33.7 us -> none  [shards(): surface = lax.all_gather(window, 'gz', axis=1, tiled=True)]
    all_to_all x0 -> x1, blocking collectives: none -> 15.6 us  [to_columns(): lax.all_to_all(stacked, ('gx', 'gz'), split_axis=3, concat_axis=2, tiled=...]
    all_to_all x4 -> x3, starting transfers between devices: 32.1 us -> 20.3 us  [to_columns(): lax.all_to_all(stacked, ('gx', 'gz'), split_axis=3, concat_axis=2, tiled=...]
    all_to_all x0 -> x1, starting transfers between devices: none -> 7.12 us  [shards(): lax.all_to_all(jnp.stack(lax.axis_size('gz') * [window], 0), 'gz', 0, 0)]
    all_to_all x4 -> x3, waiting for transfers between devices: 34.8 us -> 30.5 us  [to_columns(): lax.all_to_all(stacked, ('gx', 'gz'), split_axis=3, concat_axis=2, tiled=...]
    unnamed x80 -> x62, local copies, waits for them, and re-layouts: 133 us -> 130 us
  transfers between devices with their start and end apart: 13 -> 13, of which waited for: 8 -> 9; matrix products, arithmetic and copies ran while one was open for 27% -> 19% of each run, Pallas kernels for 0% -> 0%
where the time goes in v1:
time: 579 us; the launch traced here: 568 us
  local copies, waits for them, and re-layouts  276 us (48%)
  matrix products  63.1 us (11%)
  other arithmetic  60.3 us (10%)
  starting transfers between devices  60.3 us (10%)
  waiting for transfers between devices  58.4 us (10%)
  blocking collectives  47.4 us (8%)
    unnamed x62, local copies, waits for them, and re-layouts  130 us
    all_to_all x8, local copies, waits for them, and re-layouts, to_rows(): lax.all_to_all(stacked, ('gx', 'gz'), split_axis=2, concat_axis=3, tiled=...  57.7 us
    unnamed x15, other arithmetic  34 us
    all_to_all x9, local copies, waits for them, and re-layouts, to_columns(): lax.all_to_all(stacked, ('gx', 'gz'), split_axis=3, concat_axis=2, tiled=...  32.4 us
    all_to_all x1, blocking collectives, to_rows(): lax.all_to_all(stacked, ('gx', 'gz'), split_axis=2, concat_axis=3, tiled=...  31.8 us
    all_to_all x3, waiting for transfers between devices, to_columns(): lax.all_to_all(stacked, ('gx', 'gz'), split_axis=3, concat_axis=2, tiled=...  30.5 us
    all_to_all x3, starting transfers between devices, to_columns(): lax.all_to_all(stacked, ('gx', 'gz'), split_axis=3, concat_axis=2, tiled=...  20.3 us
    mul x5, local copies, waits for them, and re-layouts, transform_last(): real_part = real_part.reshape(leading + (length,)) * factor  20 us
  transfers between devices with their start and end apart: 13, of which 9 were waited for; matrix products, arithmetic and copies ran while one was open for 19% of the time, Pallas kernels for 0%

profile of v1, /device:TPU:8, one launch (start us, length us, event | category | flops | bytes accessed | tf_op | source)
XLA Modules:
  0.0 568.3 jit_solution(14943685306775528808)
XLA Ops:
  8.7 7.0 %fusion.923 = f32[2048,2,2,16]{3,2,1,0:T(2,128)} fusion(f32[2,1,16,2048]{2,1,0,3:T(1,128)} %bitcast.797, f32[2,1,16,2048]{2,1,0,3:T(1,128)S(1)} %bitcast.795), kind=kLoop, calls=%fused_computation.1021 | loop fusion | flops 131072 | bytes 1048576
  15.8 8.0 %reshape.1083 = f32[128,1,1024]{2,1,0:T(1,128)} reshape(f32[2048,2,2,16]{3,2,1,0:T(2,128)} %fusion.923) | data formatting | bytes 1048576
  23.7 10.8 %all-to-all-start = ((f32[128,1,1024]{2,1,0:T(1,128)}), f32[128,1,1024]{2,1,0:T(1,128)S(1)}, u32[]{:S(2)}, u32[]{:S(2)}) async-start(f32[128,1,1024]{2,1,0:T(1,128)} %reshape.1083), calls=%async_computation | async-start | bytes 1048576 | tf_op jit(solution)/shard_map/all_to_all | solution.py:114
  34.6 12.8 %all-to-all-done = f32[128,1,1024]{2,1,0:T(1,128)S(1)} async-done(((f32[128,1,1024]{2,1,0:T(1,128)}), f32[128,1,1024]{2,1,0:T(1,128)S(1)}, u32[]{:S(2)}, u32[]{:S(2)}) %all-to-all-start) | async-done | bytes 524320 | tf_op jit(solution)/shard_map/all_to_all | solution.py:114
  50.0 6.9 %reshape.1084 = f32[2048,2,2,16]{3,2,1,0:T(2,128)} reshape(f32[128,1024]{1,0:T(8,128)S(1)} %reduce) | data formatting | bytes 1048576
  56.9 6.6 %copy.542 = f32[2,2,16,128,16]{2,3,4,1,0:T(8,128)} copy(f32[2,2,16,128,16]{2,1,0,4,3:T(2,128)} %bitcast.778) | data formatting | bytes 1048576 | tf_op jit(solution)/shard_map/all_to_all | solution.py:114
  63.5 4.9 all_to_all.110
  83.3 16.8 %copy.276 = f32[7,1,16,2048]{2,1,0,3:T(1,128)} copy(f32[7,1,16,2048]{3,2,0,1:T(8,128)} %mul.3195) | data formatting | bytes 1835008 | tf_op jit(solution)/shard_map/mul | solution.py:92
  102.4 12.5 %copy.277 = f32[7,1,16,2048]{2,1,0,3:T(1,128)} copy(f32[7,1,16,2048]{3,2,0,1:T(8,128)S(1)} %mul.3198) | data formatting | bytes 1835008 | tf_op jit(solution)/shard_map/mul | solution.py:95
  114.9 19.1 %fusion.921 = f32[2048,7,2,16]{3,2,1,0:T(2,128)} fusion(f32[7,1,16,2048]{2,1,0,3:T(1,128)} %copy.277, f32[7,1,16,2048]{2,1,0,3:T(1,128)} %copy.276), kind=kLoop, calls=%fused_computation.1019 | loop fusion | flops 458752 | bytes 3670016
  134.0 22.7 %reshape.1085 = f32[128,1,3584]{2,1,0:T(1,128)} reshape(f32[2048,7,2,16]{3,2,1,0:T(2,128)} %fusion.921) | data formatting | bytes 3670016
  156.7 31.8 %all_to_all.149 = f32[128,1,3584]{2,1,0:T(1,128)S(1)} all-to-all(f32[128,1,3584]{2,1,0:T(1,128)} %reshape.1085), channel_id=1, replica_groups=mesh['gx'=16,'gz'=8] {'gx','gz'}, dimensions={0} | all-to-all | bytes 3670016 | tf_op jit(solution)/shard_map/all_to_all | solution.py:118
  188.5 6.7 %reduce.1 = f32[128,3584]{1,0:T(8,128)} reduce(f32[128,1,3584]{2,1,0:T(1,128)S(1)} %all_to_all.149, f32[]{:T(128)} %broadcast.1810), dimensions={1}, to_apply=%all_to_all.111.reduce_sub_computation | reduce | bytes 3670020 | tf_op jit(solution)/shard_map/all_to_all | solution.py:118
  195.2 22.7 %reshape.1086 = f32[2048,7,2,16]{3,2,1,0:T(2,128)} reshape(f32[128,3584]{1,0:T(8,128)} %reduce.1) | data formatting | bytes 3670016
  217.9 18.8 %copy.540 = f32[7,2,128,16,16]{4,2,3,1,0:T(8,128)} copy(f32[7,2,128,16,16]{4,1,0,3,2:T(2,128)} %bitcast.776) | data formatting | bytes 3670016 | tf_op jit(solution)/shard_map/all_to_all | solution.py:118
  236.7 13.0 %all_to_all.114 = f32[7,2,16,2048]{3,2,1,0:T(8,128)S(1)} reshape(f32[7,2,16,128,16]{4,3,2,1,0:T(8,128)} %bitcast.777) | data formatting | bytes 3670016 | tf_op jit(solution)/shard_map/all_to_all | solution.py:118
  261.4 2.9 reshape.1087
  264.3 15.6 %all_to_all.150 = f32[128,1,512]{2,1,0:T(1,128)S(1)} all-to-all(f32[128,1,512]{2,1,0:T(1,128)S(1)} %reshape.1087), channel_id=1, replica_groups=mesh['gx'=16,'gz'=8] {'gx','gz'}, dimensions={0} | all-to-all | bytes 524288 | tf_op jit(solution)/shard_map/all_to_all | solution.py:114
  281.2 2.8 reshape.1088
  284.0 2.6 copy.547
  286.5 3.1 all_to_all.118
  300.9 2.6 copy.403
  303.5 7.0 %fusion.922 = f32[2048,2,2,16]{3,2,1,0:T(2,128)} fusion(f32[2,1,16,2048]{2,1,0,3:T(1,128)} %bitcast.798, f32[2,1,16,2048]{2,1,0,3:T(1,128)S(1)} %bitcast.796), kind=kLoop, calls=%fused_computation.1020 | loop fusion | flops 131072 | bytes 1048576
  310.5 8.0 %reshape.1089 = f32[128,1,1024]{2,1,0:T(1,128)} reshape(f32[2048,2,2,16]{3,2,1,0:T(2,128)} %fusion.922) | data formatting | bytes 1048576
  318.5 4.9 all-to-all-start.3
  324.1 3.6 collective-permute-start
  331.1 5.5 all-to-all-done.3
  338.5 7.3 %reshape.1090 = f32[2048,2,2,16]{3,2,1,0:T(2,128)} reshape(f32[128,1024]{1,0:T(8,128)S(1)} %reduce.3) | data formatting | bytes 1048576
  345.8 6.6 %copy.541 = f32[2,2,128,16,16]{4,2,3,1,0:T(8,128)} copy(f32[2,2,128,16,16]{4,1,0,3,2:T(2,128)} %bitcast.780) | data formatting | bytes 1048576 | tf_op jit(solution)/shard_map/all_to_all | solution.py:118
  352.4 4.7 all_to_all.122
  363.7 2.3 copy.307
  366.0 5.2 reshape.1091
  371.1 4.7 all-to-all-start.4
  376.4 10.0 %all-to-all-done.4 = f32[128,1,512]{2,1,0:T(1,128)S(1)} async-done(((f32[128,1,512]{2,1,0:T(1,128)}), f32[128,1,512]{2,1,0:T(1,128)S(1)}, u32[]{:S(2)}, u32[]{:S(2)}) %all-to-all-start.4) | async-done | bytes 262176 | tf_op jit(solution)/shard_map/all_to_all | solution.py:114
  387.7 4.1 reshape.1092
  391.8 4.1 copy.546
  396.0 3.1 all_to_all.126
  406.1 2.3 copy.318
  408.3 2.6 bitcast_bitcast_fusion.1
  411.0 5.4 reshape.1093
  416.4 4.8 all-to-all-start.5
  422.3 9.3 %all-to-all-done.5 = f32[128,1,512]{2,1,0:T(1,128)S(1)} async-done(((f32[128,1,512]{2,1,0:T(1,128)}), f32[128,1,512]{2,1,0:T(1,128)S(1)}, u32[]{:S(2)}, u32[]{:S(2)}) %all-to-all-start.5) | async-done | bytes 262176 | tf_op jit(solution)/shard_map/all_to_all | solution.py:118
  433.0 4.1 reshape.1094
  437.1 4.1 copy.545
  441.3 3.1 all_to_all.130
  452.9 5.1 reshape.1095
  458.0 4.8 all-to-all-start.6
  462.9 2.8 fusion.48
  465.6 7.7 %all-to-all-done.6 = f32[128,1,512]{2,1,0:T(1,128)S(1)} async-done(((f32[128,1,512]{2,1,0:T(1,128)}), f32[128,1,512]{2,1,0:T(1,128)S(1)}, u32[]{:S(2)}, u32[]{:S(2)}) %all-to-all-start.6) | async-done | bytes 262176 | tf_op jit(solution)/shard_map/all_to_all | solution.py:114
  474.7 4.1 reshape.1096
  478.8 4.1 copy.544
  482.9 3.1 all_to_all.134
  495.3 2.6 bitcast_bitcast_fusion
  497.9 5.2 reshape.1097
  503.1 4.8 all-to-all-start.7
  508.7 5.3 collective-permute-start.2
  519.9 4.1 reshape.1098
  524.1 4.1 copy.543
  528.2 3.1 all_to_all.138
  535.0 7.1 %all-to-all-start.8 = ((f32[8,3,16,256]{3,2,1,0:T(8,128)}), f32[8,3,16,256]{3,2,1,0:T(8,128)S(1)}, u32[]{:S(2)}, u32[]{:S(2)}) async-start(f32[8,3,16,256]{3,2,1,0:T(8,128)} %stack.113), calls=%async_computation.8 | async-start | bytes 786432 | tf_op jit(solution)/shard_map/all_to_all | solution.py:226
  544.9 4.9 all-to-all-done.8
  551.8 4.4 collective-permute-start.4
  556.2 3.0 collective-permute-start.5
  560.2 5.3 collective-permute-done.5
  (251 shorter events, 111.9 us)
Async XLA Ops:
  23.7 23.7 %all-to-all-start = ((f32[128,1,1024]{2,1,0:T(1,128)}), f32[128,1,1024]{2,1,0:T(1,128)S(1)}, u32[]{:S(2)}, u32[]{:S(2)}) async-start(f32[128,1,1024]{2,1,0:T(1,128)} %reshape.1083), calls=%async_computation | async-start | bytes 1048576 | tf_op jit(solution)/shard_map/all_to_all | solution.py:114
  255.6 1.8 copy-start.1
  318.5 18.0 %all-to-all-start.3 = ((f32[128,1,1024]{2,1,0:T(1,128)}), f32[128,1,1024]{2,1,0:T(1,128)S(1)}, u32[]{:S(2)}, u32[]{:S(2)}) async-start(f32[128,1,1024]{2,1,0:T(1,128)} %reshape.1089), calls=%async_computation.3 | async-start | bytes 1048576 | tf_op jit(solution)/shard_map/all_to_all | solution.py:118
  324.1 138.8 %collective-permute-start = (f32[1,8,256]{2,0,1:T(1,128)S(1)}, f32[1,8,256]{2,0,1:T(1,128)S(1)}, u32[]{:S(2)}, u32[]{:S(2)}) collective-permute-start(f32[1,8,256]{2,0,1:T(1,128)S(1)} %copy.322), channel_id=1, source_target_pairs={{8,0},{16,8},{24,16},{32,24},{40,32},{48,40},{56,48},{64,56},{72,6... | collective-permute-start | bytes 24584 | tf_op jit(solution)/shard_map/ppermute | solution.py:23
  327.7 135.1 %collective-permute-start.1 = (f32[1,8,256]{2,0,1:T(1,128)S(1)}, f32[1,8,256]{2,0,1:T(1,128)S(1)}, u32[]{:S(2)}, u32[]{:S(2)}) collective-permute-start(f32[1,8,256]{2,0,1:T(1,128)S(1)} %copy.324), channel_id=1, source_target_pairs={{0,8},{8,16},{16,24},{24,32},{32,40},{40,48},{48,56},{56,64},{64,7... | collective-permute-start | bytes 24584 | tf_op jit(solution)/shard_map/ppermute | solution.py:22
  371.1 15.3 %all-to-all-start.4 = ((f32[128,1,512]{2,1,0:T(1,128)}), f32[128,1,512]{2,1,0:T(1,128)S(1)}, u32[]{:S(2)}, u32[]{:S(2)}) async-start(f32[128,1,512]{2,1,0:T(1,128)} %reshape.1091), calls=%async_computation.4 | async-start | bytes 524288 | tf_op jit(solution)/shard_map/all_to_all | solution.py:114
  416.4 15.3 %all-to-all-start.5 = ((f32[128,1,512]{2,1,0:T(1,128)}), f32[128,1,512]{2,1,0:T(1,128)S(1)}, u32[]{:S(2)}, u32[]{:S(2)}) async-start(f32[128,1,512]{2,1,0:T(1,128)} %reshape.1093), calls=%async_computation.5 | async-start | bytes 524288 | tf_op jit(solution)/shard_map/all_to_all | solution.py:118
  444.4 2.8 copy-start.3
  444.4 2.8 copy-start.4
  444.4 2.8 copy-start.5
  447.6 3.0 copy-start.2
  450.6 12.3 %copy-start = (f32[128,8,256]{2,1,0:T(8,128)S(1)}, f32[128,8,256]{2,1,0:T(8,128)}, u32[]{:S(2)}) copy-start(f32[128,8,256]{2,1,0:T(8,128)} %param.7) | copy-start | bytes 3145732
  458.0 15.3 %all-to-all-start.6 = ((f32[128,1,512]{2,1,0:T(1,128)}), f32[128,1,512]{2,1,0:T(1,128)S(1)}, u32[]{:S(2)}, u32[]{:S(2)}) async-start(f32[128,1,512]{2,1,0:T(1,128)} %reshape.1095), calls=%async_computation.6 | async-start | bytes 524288 | tf_op jit(solution)/shard_map/all_to_all | solution.py:114
  503.1 15.5 %all-to-all-start.7 = ((f32[128,1,512]{2,1,0:T(1,128)}), f32[128,1,512]{2,1,0:T(1,128)S(1)}, u32[]{:S(2)}, u32[]{:S(2)}) async-start(f32[128,1,512]{2,1,0:T(1,128)} %reshape.1097), calls=%async_computation.7 | async-start | bytes 524288 | tf_op jit(solution)/shard_map/all_to_all | solution.py:118
  508.7 34.6 %collective-permute-start.2 = (f32[128,1,256]{2,0,1:T(8,128)}, f32[128,1,256]{2,0,1:T(8,128)S(1)}, u32[]{:S(2)}, u32[]{:S(2)}) collective-permute-start(f32[128,1,256]{2,0,1:T(8,128)} %get-tuple-element.20), channel_id=1, source_target_pairs={{1,0},{2,1},{3,2},{4,3},{5,4},{6,5},{7,6},{9,8},{10,9},{11,10},{12... | collective-permute-start | bytes 393224 | tf_op jit(solution)/shard_map/ppermute | solution.py:23
  514.0 29.2 %collective-permute-start.3 = (f32[128,1,256]{2,0,1:T(8,128)}, f32[128,1,256]{2,0,1:T(8,128)}, u32[]{:S(2)}, u32[]{:S(2)}) collective-permute-start(f32[128,1,256]{2,0,1:T(8,128)} %get-tuple-element.21), channel_id=1, source_target_pairs={{0,1},{1,2},{2,3},{3,4},{4,5},{5,6},{6,7},{8,9},{9,10},{10,11},{11... | collective-permute-start | bytes 393224 | tf_op jit(solution)/shard_map/ppermute | solution.py:22
  535.0 14.8 %all-to-all-start.8 = ((f32[8,3,16,256]{3,2,1,0:T(8,128)}), f32[8,3,16,256]{3,2,1,0:T(8,128)S(1)}, u32[]{:S(2)}, u32[]{:S(2)}) async-start(f32[8,3,16,256]{3,2,1,0:T(8,128)} %stack.113), calls=%async_computation.8 | async-start | bytes 786432 | tf_op jit(solution)/shard_map/all_to_all | solution.py:226
  542.1 7.8 %copy-start.6 = (f32[8]{0:T(128)S(1)}, f32[8]{0:T(128)}, u32[]{:S(2)}) copy-start(f32[8]{0:T(128)} %multiply_subtract_fusion.18) | copy-start | bytes 100
  551.8 8.4 %collective-permute-start.4 = (f32[128,1,256]{2,0,1:T(8,128)S(1)}, f32[128,1,256]{2,0,1:T(8,128)S(1)}, u32[]{:S(2)}, u32[]{:S(2)}) collective-permute-start(f32[128,1,256]{2,0,1:T(8,128)S(1)} %get-tuple-element.14), channel_id=1, source_target_pairs={{1,0},{2,1},{3,2},{4,3},{5,4},{6,5},{7,6},{9,8},{10,9},{11,10},{12... | collective-permute-start | bytes 393224 | tf_op jit(solution)/shard_map/ppermute | solution.py:23
  556.2 9.3 %collective-permute-start.5 = (f32[128,1,256]{2,0,1:T(8,128)S(1)}, f32[128,1,256]{2,0,1:T(8,128)S(1)}, u32[]{:S(2)}, u32[]{:S(2)}) collective-permute-start(f32[128,1,256]{2,0,1:T(8,128)S(1)} %get-tuple-element.15), channel_id=1, source_target_pairs={{0,1},{1,2},{2,3},{3,4},{4,5},{5,6},{6,7},{8,9},{9,10},{10,11},{11... | collective-permute-start | bytes 393224 | tf_op jit(solution)/shard_map/ppermute | solution.py:22
